TPU v7x, 512 devices: a whole 4x8x8 slice. The times are simulated.
512 devices in a mesh: leaf: 128 (over y, z, core), sub: 4 (over x).
Axes of the slice: x: 4, y: 8, z: 8, core: 2. Of those that a mesh axis runs over, the one named last changes fastest.
Arguments:
- field: float32 [64, 524288], P(None, ('leaf', 'sub')), may hold values from -6 to 6
- coords: float32 [3, 524288], P(None, ('leaf', 'sub')), may hold values from -6 to 6
- basis: float32 [2048, 64, 256], P(('leaf', 'sub')), may hold values from -0.375 to 0.375
- up_transfer: float32 [2048, 64, 64], P(('leaf', 'sub')), may hold values from -0.1875 to 0.1875
- down_transfer: float32 [2048, 64, 64], P(('leaf', 'sub')), may hold values from -0.75 to 0.75
- couplings: float32 [16384, 64, 64], P(('leaf', 'sub')), may hold values from -0.25 to 0.25
- top_coupling: float32 [128, 128, 64, 64], P('leaf', None, 'sub'), may hold values from -0.25 to 0.25
- send_leaf: int32 [128, 4, 128, 1], P('leaf', 'sub'), may hold values from 0 to 3
- list_slot: int32 [2048, 8], P(('leaf', 'sub')), may hold values from 0 to 127, as said below
- list_block: int32 [2048, 8], P(('leaf', 'sub')), may hold values from 0 to 31
Outputs:
- result: float32 [64, 524288], P(None, ('leaf', 'sub'))
Inputs may be any that keep to these rules, and one draw needn't show every extreme that they name: send_leaf[e, s, d, c] is the leaf, among the 4 of device (e, s), whose skeleton fills slot c of what that device sends to device (d, s). `list_slot`: a list entry q names slot q % 1 from the device q // 1 of the leaf axis with the same sub index; where a device's 4 * 8 list entries are at least 128, every slot is named by some entry of that device, else the device's entries are all different. `list_block`: a list entry names one of the 32 coupling blocks of the leaf's own device.
All inputs are finite; a program needn't handle non-finite values.
Results may differ from a plain program's by a relative error of at most 0.0001.
Values sent between devices are 32-bit elements; how exact they have to be, the bound alone decides.
A program may use at most 64 MiB of HBM per device.

v0:
```python
import math
import jax
import jax.numpy as jnp
from jax import lax
from jax.sharding import PartitionSpec as P

highest = lax.Precision.HIGHEST


def extended(block, sides, width):
    for axis, dim in sides:
        count = lax.axis_size(axis)
        forward = [(i, i + 1) for i in range(count - 1)]
        backward = [(target, source) for source, target in forward]
        low = lax.ppermute(
            lax.slice_in_dim(block, block.shape[dim] - width, None, axis=dim), axis, forward
        )
        high = lax.ppermute(lax.slice_in_dim(block, 0, width, axis=dim), axis, backward)
        block = jnp.concatenate([low, block, high], axis=dim)
    return block


def kernel_block(source_points, target_points, leaf_size):
    dist = jnp.zeros((source_points.shape[1], target_points.shape[1]), jnp.float32)
    for component in range(3):
        gap = source_points[component][:, None] - target_points[component][None, :]
        dist = dist + gap * gap
    return jnp.exp(-0.5 * dist) * (1.0 / math.sqrt(leaf_size))


def add_top(rows, coupling_rows):
    return jnp.einsum("epr,erq->pq", rows, coupling_rows, precision=highest)


def far_terms(incoming, list_slot, chosen, rows, rank):
    gathered = incoming.reshape(-1, rows, rank)[list_slot]
    return jnp.einsum("lkpr,lkrq->lpq", gathered, chosen, precision=highest)


def one_product(
    field,
    coords,
    basis,
    up_transfer,
    down_transfer,
    couplings,
    top_coupling,
    send_leaf,
    list_slot,
    list_block,
):
    rhs_count = field.shape[0]
    leaf_count = basis.shape[0]
    rank = basis.shape[1]
    leaf_size = basis.shape[2]
    stacked = jnp.concatenate([field, coords], 0)
    padded = extended(stacked, ((("leaf", "sub"), 1),), leaf_size)
    leaf_field = field.reshape(rhs_count, leaf_count, leaf_size)
    skeleton = jnp.einsum("pla,lra->lpr", leaf_field, basis, precision=highest)
    outgoing = skeleton[send_leaf.reshape(-1)]
    slot_total = outgoing.shape[0]
    chosen = couplings[list_block]
    incoming = lax.all_to_all(
        outgoing.reshape(slot_total, rhs_count * rank),
        "leaf",
        split_axis=0,
        concat_axis=0,
        tiled=True,
    )
    far = far_terms(incoming, list_slot, chosen, rhs_count, rank)

    def near_leaf(position):
        window = lax.dynamic_slice_in_dim(padded, position * leaf_size, 3 * leaf_size, 1)
        own_points = lax.dynamic_slice_in_dim(
            padded[rhs_count:], (position + 1) * leaf_size, leaf_size, 1
        )
        kernels = kernel_block(window[rhs_count:], own_points, leaf_size)
        return jnp.dot(
            window[:rhs_count], kernels, precision=highest, preferred_element_type=jnp.float32
        )

    near = lax.map(near_leaf, jnp.arange(leaf_count, dtype=jnp.int32))
    parent_part = jnp.einsum("lpr,lrq->pq", skeleton, up_transfer, precision=highest)
    quarter = top_coupling.shape[2]
    coupling_rows = top_coupling[0]
    parent = lax.psum(parent_part, "sub")
    row_start = lax.axis_index("sub") * quarter
    rows = lax.dynamic_slice_in_dim(
        lax.all_gather(parent[None], "leaf", axis=0, tiled=True), row_start, quarter, 2
    )
    top_partial = add_top(rows, coupling_rows)
    top_term = lax.psum(top_partial, "sub")
    coef = far + jnp.einsum("pr,lrq->lpq", top_term, down_transfer, precision=highest)
    total = near + jnp.einsum("lpr,lra->lpa", coef, basis, precision=highest)
    return total.transpose(1, 0, 2).reshape(rhs_count, leaf_count * leaf_size)


def local(
    field,
    coords,
    basis,
    up_transfer,
    down_transfer,
    couplings,
    top_coupling,
    send_leaf,
    list_slot,
    list_block,
):
    current = field
    for repeat in range(2):
        current = one_product(
            current,
            coords,
            basis,
            up_transfer,
            down_transfer,
            couplings,
            top_coupling,
            send_leaf,
            list_slot,
            list_block,
        )
    return current


def solution(mesh):
    in_specs = (
        P(None, ("leaf", "sub")),
        P(None, ("leaf", "sub")),
        P(("leaf", "sub"), None, None),
        P(("leaf", "sub"), None, None),
        P(("leaf", "sub"), None, None),
        P(("leaf", "sub"), None, None),
        P("leaf", None, "sub", None),
        P("leaf", "sub", None, None),
        P(("leaf", "sub"), None),
        P(("leaf", "sub"), None),
    )
    out_specs = P(None, ("leaf", "sub"))
    return jax.shard_map(local, mesh=mesh, in_specs=in_specs, out_specs=out_specs, check_vma=False)
```

profile of v0, /device:TPU:16, one launch (start us, length us, event | category | flops | bytes accessed | tf_op | source)
XLA Modules:
  0.0 379.2 jit_solution(1473924243727374704)
XLA Ops:
  6.5 1.5 fusion.52
  8.0 1.2 convolution_bitcast_fusion.9
  9.2 17.7 %psum.28 = f32[1,64,64]{2,1,0:T(8,128)} all-reduce(f32[1,64,64]{2,1,0:T(8,128)S(1)} %convolution_bitcast_fusion.9), channel_id=1, replica_groups=mesh['leaf'=128,'sub'=4] {'sub'}, use_global_device_ids=true, to_apply=%region_2.3 | all-reduce | flops 4096 | bytes 32768 | tf_op jit(solution)/shard_map/psum | solution.py:86
  26.9 0.7 fusion.60
  27.6 0.6 copy-done.12
  28.2 2.8 gather_fusion
  31.0 3.8 copy.27
  34.8 4.1 %copy.28 = f32[128,1,4096]{2,1,0:T(1,128)} copy(f32[128,1,4096]{0,2,1:T(8,128)S(1)} %bitcast.122) | data formatting | bytes 4194304 | tf_op jit(solution)/shard_map/all_to_all | solution.py:63
  38.9 17.8 %all-to-all-start = ((f32[128,1,4096]{2,1,0:T(1,128)}), f32[128,1,4096]{2,1,0:T(1,128)}, u32[]{:S(2)}, u32[]{:S(2)}) async-start(f32[128,1,4096]{2,1,0:T(1,128)} %copy.28), calls=%async_computation | async-start | bytes 4194304 | tf_op jit(solution)/shard_map/all_to_all | solution.py:63
  56.8 1.9 collective-permute-start
  58.8 7.9 %collective-permute-start.1 = (f32[67,256]{1,0:T(8,128)S(1)}, f32[67,256]{1,0:T(8,128)S(1)}, u32[]{:S(2)}, u32[]{:S(2)}) collective-permute-start(f32[67,256]{1,0:T(8,128)S(1)} %get-tuple-element.82), channel_id=1, source_target_pairs={{1,0},{2,1},{3,2},{4,3},{5,4},{6,5},{7,6},{8,7},{9,8},{10,9},{11,1... | collective-permute-start | bytes 205832 | tf_op jit(solution)/shard_map/ppermute | solution.py:18
  66.8 0.6 pad_clamp_fusion
  67.4 0.6 gather_fusion.2
  68.0 36.9 %collective-permute-done = f32[67,256]{1,0:T(8,128)S(1)} collective-permute-done((f32[67,256]{1,0:T(8,128)S(1)}, f32[67,256]{1,0:T(8,128)S(1)}, u32[]{:S(2)}, u32[]{:S(2)}) %collective-permute-start) | collective-permute-done | bytes 68640 | tf_op jit(solution)/shard_map/ppermute | solution.py:15
  105.0 11.9 %while.20 = (s32[]{:T(128)}, f32[4,64,256]{2,1,0:T(8,128)S(1)}, s32[4]{0:T(128)S(1)}, f32[67,1536]{1,0:T(8,128)S(1)}, s32[]{:T(128)}, /*index=5*/s32[1]{0:T(128)...) while((s32[]{:T(128)}, f32[4,64,256]{2,1,0:T(8,128)S(1)}, ...), condition=%wide.region_1.2_spmd, body=%wide.region_0.1_spmd.sunk | while | flops 152961040 | bytes 339289 | solution.py:82
  105.1 0.6 dynamic_slice.31
  107.1 0.9 fusion.91
  108.0 0.6 dynamic_slice.31
  110.1 0.9 fusion.91
  111.0 0.6 dynamic_slice.31
  113.1 0.9 fusion.91
  114.0 0.6 dynamic_slice.31
  116.1 0.9 fusion.91
  117.0 32.6 %all-gather.3.cloned.1.call-done = f32[128,64,64]{2,1,0:T(8,128)} async-done(((f32[1,64,64]{2,1,0:T(8,128)}), f32[128,64,64]{2,1,0:T(8,128)}) %all-gather.3.cloned.1.call-update) | async-done | bytes 2097168 | tf_op jit(solution)/shard_map/all_gather | solution.py:89
  149.6 5.3 %constant_dynamic-slice_fusion.3 = f32[128,64,16]{2,1,0:T(8,128)} fusion(f32[128,64,64]{2,1,0:T(8,128)} %all-gather.3.cloned.1.call-done, s32[]{:T(128)S(6)} %select_n.38), kind=kLoop, calls=%fused_computation.99 | loop fusion | bytes 1048580 | tf_op jit(solution)/shard_map/dynamic_slice | solution.py:88
  154.9 4.0 %copy.41 = f32[128,64,16]{0,1,2:T(8,128)S(1)} copy(f32[128,64,16]{2,1,0:T(8,128)} %constant_dynamic-slice_fusion.3) | data formatting | bytes 1048576
  159.0 0.6 convolution_bitcast_fusion.8
  159.5 17.6 %psum.29 = f32[64,64]{1,0:T(8,128)} all-reduce(f32[64,64]{1,0:T(8,128)S(1)} %convolution_bitcast_fusion.8), channel_id=1, replica_groups=mesh['leaf'=128,'sub'=4] {'sub'}, use_global_device_ids=true, to_apply=%region_3.4 | all-reduce | flops 4096 | bytes 32768 | tf_op jit(solution)/shard_map/psum | solution.py:92
  177.1 5.6 %copy.29 = f32[128,1,4096]{0,2,1:T(8,128)} copy(f32[128,1,4096]{2,1,0:T(1,128)} %all-to-all-done) | data formatting | bytes 4194304 | tf_op jit(solution)/shard_map/all_to_all | solution.py:63
  182.8 5.6 %copy.30 = f32[128,64,64]{2,1,0:T(8,128)} copy(f32[128,64,64]{0,2,1:T(8,128)} %bitcast.123) | data formatting | bytes 4194304 | tf_op jit(solution)/shard_map/reshape | solution.py:36
  188.4 2.9 gather_fusion.1
  191.3 1.1 convolution_bitcast_fusion.5
  192.4 1.0 fusion.49
  193.8 1.3 fusion.55
  195.2 1.2 convolution_bitcast_fusion.7
  196.4 15.0 %psum.30 = f32[1,64,64]{2,1,0:T(8,128)} all-reduce(f32[1,64,64]{2,1,0:T(8,128)S(1)} %convolution_bitcast_fusion.7), channel_id=1, replica_groups=mesh['leaf'=128,'sub'=4] {'sub'}, use_global_device_ids=true, to_apply=%region_6.7 | all-reduce | flops 4096 | bytes 32768 | tf_op jit(solution)/shard_map/psum | solution.py:86
  211.4 2.9 gather_fusion.3
  214.4 4.7 %copy.33 = f32[128,64,64]{0,2,1:T(8,128)} copy(f32[128,64,64]{2,1,0:T(8,128)} %gather_fusion.3) | data formatting | bytes 4194304 | tf_op jit(solution)/shard_map/gather | solution.py:60
  219.1 5.7 %copy.34 = f32[128,1,4096]{2,1,0:T(1,128)} copy(f32[128,1,4096]{0,2,1:T(8,128)} %bitcast.124) | data formatting | bytes 4194304 | tf_op jit(solution)/shard_map/all_to_all | solution.py:63
  224.8 10.4 %all-to-all-start.1 = ((f32[128,1,4096]{2,1,0:T(1,128)}), f32[128,1,4096]{2,1,0:T(1,128)}, u32[]{:S(2)}, u32[]{:S(2)}) async-start(f32[128,1,4096]{2,1,0:T(1,128)} %copy.34), calls=%async_computation.1 | async-start | bytes 4194304 | tf_op jit(solution)/shard_map/all_to_all | solution.py:63
  235.4 2.6 collective-permute-start.2
  238.0 7.2 %collective-permute-start.3 = (f32[67,256]{1,0:T(8,128)S(1)}, f32[67,256]{1,0:T(8,128)S(1)}, u32[]{:S(2)}, u32[]{:S(2)}) collective-permute-start(f32[67,256]{1,0:T(8,128)S(1)} %get-tuple-element.80), channel_id=1, source_target_pairs={{1,0},{2,1},{3,2},{4,3},{5,4},{6,5},{7,6},{8,7},{9,8},{10,9},{11,1... | collective-permute-start | bytes 205832 | tf_op jit(solution)/shard_map/ppermute | solution.py:18
  245.1 40.4 %collective-permute-done.2 = f32[67,256]{1,0:T(8,128)S(1)} collective-permute-done((f32[67,256]{1,0:T(8,128)S(1)}, f32[67,256]{1,0:T(8,128)S(1)}, u32[]{:S(2)}, u32[]{:S(2)}) %collective-permute-start.2) | collective-permute-done | bytes 68640 | tf_op jit(solution)/shard_map/ppermute | solution.py:15
  285.6 11.9 %while.21 = (s32[]{:T(128)}, f32[4,64,256]{2,1,0:T(8,128)S(1)}, s32[4]{0:T(128)S(1)}, f32[67,1536]{1,0:T(8,128)S(1)}, s32[]{:T(128)}, /*index=5*/s32[1]{0:T(128)...) while((s32[]{:T(128)}, f32[4,64,256]{2,1,0:T(8,128)S(1)}, ...), condition=%wide.region_5.6_spmd, body=%wide.region_4.5_spmd.sunk | while | flops 152961040 | bytes 339289 | solution.py:82
  285.6 0.6 dynamic_slice.32
  287.7 0.9 fusion.94
  288.6 0.6 dynamic_slice.32
  290.7 0.9 fusion.94
  291.6 0.6 dynamic_slice.32
  293.6 0.9 fusion.94
  294.6 0.6 dynamic_slice.32
  296.6 0.9 fusion.94
  297.6 29.0 %all-gather.5.cloned.1.call-done = f32[128,64,64]{2,1,0:T(8,128)} async-done(((f32[1,64,64]{2,1,0:T(8,128)}), f32[128,64,64]{2,1,0:T(8,128)}) %all-gather.5.cloned.1.call-update) | async-done | bytes 2097168 | tf_op jit(solution)/shard_map/all_gather | solution.py:89
  326.5 5.3 %constant_dynamic-slice_fusion.2 = f32[128,64,16]{2,1,0:T(8,128)} fusion(f32[128,64,64]{2,1,0:T(8,128)} %all-gather.5.cloned.1.call-done, s32[]{:T(128)S(6)} %select_n.38), kind=kLoop, calls=%fused_computation.98 | loop fusion | bytes 1048580 | tf_op jit(solution)/shard_map/dynamic_slice | solution.py:88
  331.8 4.0 %copy.42 = f32[128,64,16]{0,1,2:T(8,128)S(1)} copy(f32[128,64,16]{2,1,0:T(8,128)} %constant_dynamic-slice_fusion.2) | data formatting | bytes 1048576
  335.9 0.6 convolution_bitcast_fusion.6
  336.4 17.6 %psum.31 = f32[64,64]{1,0:T(8,128)} all-reduce(f32[64,64]{1,0:T(8,128)S(1)} %convolution_bitcast_fusion.6), channel_id=1, replica_groups=mesh['leaf'=128,'sub'=4] {'sub'}, use_global_device_ids=true, to_apply=%region_7.8 | all-reduce | flops 4096 | bytes 32768 | tf_op jit(solution)/shard_map/psum | solution.py:92
  354.0 5.6 %copy.35 = f32[128,1,4096]{0,2,1:T(8,128)} copy(f32[128,1,4096]{2,1,0:T(1,128)} %all-to-all-done.1) | data formatting | bytes 4194304 | tf_op jit(solution)/shard_map/all_to_all | solution.py:63
  359.7 5.6 %copy.36 = f32[128,64,64]{2,1,0:T(8,128)} copy(f32[128,64,64]{0,2,1:T(8,128)} %bitcast.125) | data formatting | bytes 4194304 | tf_op jit(solution)/shard_map/reshape | solution.py:36
  365.3 2.8 gather_fusion.4
  368.1 1.1 convolution_bitcast_fusion.4
  369.2 1.0 fusion.48
  370.6 1.0 add_bitcast_fusion
  371.6 0.7 copy.45
  (82 shorter events, 2.8 us)
Async XLA Ops:
  6.5 60.9 %copy-start = (f32[32,64,64]{2,1,0:T(8,128)S(1)}, f32[32,64,64]{2,1,0:T(8,128)}, u32[]{:S(2)}) copy-start(f32[32,64,64]{2,1,0:T(8,128)} %param.19) | copy-start | bytes 1572868
  6.5 143.1 %all-gather.3.cloned.1.call-start = ((), (), s32[]{:S(2)}) async-start(), calls=%async_computation.2 | async-start | bytes 4227072 | tf_op jit(solution)/shard_map/all_gather | solution.py:89
  27.6 0.6 copy-start.12
  34.8 22.0 %copy-start.7 = (f32[64,1024]{1,0:T(8,128)S(1)}, f32[64,1024]{1,0:T(8,128)}, u32[]{:S(2)}) copy-start(f32[64,1024]{1,0:T(8,128)} %param.14) | copy-start | bytes 786436
  34.8 22.0 %copy-start.10 = (f32[3,1024]{1,0:T(4,128)S(1)}, f32[3,1024]{1,0:T(4,128)}, u32[]{:S(2)}) copy-start(f32[3,1024]{1,0:T(4,128)} %param.15) | copy-start | bytes 36868
  34.8 31.8 %copy-start.13 = (s32[4,8]{1,0:T(4,128)S(1)}, s32[4,8]{1,0:T(4,128)}, u32[]{:S(2)}) copy-start(s32[4,8]{1,0:T(4,128)} %param.22) | copy-start | bytes 388
  34.8 31.9 %copy-start.14 = (s32[4,8]{1,0:T(4,128)S(1)}, s32[4,8]{1,0:T(4,128)}, u32[]{:S(2)}) copy-start(s32[4,8]{1,0:T(4,128)} %param.23) | copy-start | bytes 388
  38.9 138.2 %all-to-all-start = ((f32[128,1,4096]{2,1,0:T(1,128)}), f32[128,1,4096]{2,1,0:T(1,128)}, u32[]{:S(2)}, u32[]{:S(2)}) async-start(f32[128,1,4096]{2,1,0:T(1,128)} %copy.28), calls=%async_computation | async-start | bytes 4194304 | tf_op jit(solution)/shard_map/all_to_all | solution.py:63
  56.7 269.8 %all-gather.5.cloned.1.call-start = ((), (), s32[]{:S(2)}) async-start(), calls=%async_computation.3 | async-start | bytes 4227072 | tf_op jit(solution)/shard_map/all_gather | solution.py:89
  56.8 48.1 %collective-permute-start = (f32[67,256]{1,0:T(8,128)S(1)}, f32[67,256]{1,0:T(8,128)S(1)}, u32[]{:S(2)}, u32[]{:S(2)}) collective-permute-start(f32[67,256]{1,0:T(8,128)S(1)} %get-tuple-element.81), channel_id=1, source_target_pairs={{0,1},{1,2},{2,3},{3,4},{4,5},{5,6},{6,7},{7,8},{8,9},{9,10},{10,1... | collective-permute-start | bytes 205832 | tf_op jit(solution)/shard_map/ppermute | solution.py:15
  58.8 46.2 %collective-permute-start.1 = (f32[67,256]{1,0:T(8,128)S(1)}, f32[67,256]{1,0:T(8,128)S(1)}, u32[]{:S(2)}, u32[]{:S(2)}) collective-permute-start(f32[67,256]{1,0:T(8,128)S(1)} %get-tuple-element.82), channel_id=1, source_target_pairs={{1,0},{2,1},{3,2},{4,3},{5,4},{6,5},{7,6},{8,7},{9,8},{10,9},{11,1... | collective-permute-start | bytes 205832 | tf_op jit(solution)/shard_map/ppermute | solution.py:18
  117.0 37.9 %copy-start.2 = (f32[4,64,256]{2,1,0:T(8,128)}, f32[4,64,256]{2,1,0:T(8,128)S(1)}, u32[]{:S(2)}) copy-start(f32[4,64,256]{2,1,0:T(8,128)S(1)} %get-tuple-element.49) | copy-start | bytes 786436
  154.9 4.0 %copy-start.4 = (f32[1,128,16,64]{1,3,2,0:T(8,128)S(1)}, f32[1,128,16,64]{1,3,2,0:T(8,128)}, u32[]{:S(2)}) copy-start(f32[1,128,16,64]{1,3,2,0:T(8,128)} %param.20) | copy-start | bytes 1572868
  182.8 9.7 %copy-start.8 = (f32[4,64,64]{2,1,0:T(8,128)S(1)}, f32[4,64,64]{2,1,0:T(8,128)}, u32[]{:S(2)}) copy-start(f32[4,64,64]{2,1,0:T(8,128)} %param.18) | copy-start | bytes 196612
  182.8 10.7 %copy-start.1 = (f32[4,64,256]{2,1,0:T(8,128)S(1)}, f32[4,64,256]{2,1,0:T(8,128)}, u32[]{:S(2)}) copy-start(f32[4,64,256]{2,1,0:T(8,128)} %param.16) | copy-start | bytes 786436
  219.1 16.1 %copy-start.3 = (f32[4,64,256]{2,1,0:T(8,128)S(1)}, f32[4,64,256]{2,1,0:T(8,128)}, u32[]{:S(2)}) copy-start(f32[4,64,256]{2,1,0:T(8,128)} %copy-done.2) | copy-start | bytes 786436
  224.8 129.2 %all-to-all-start.1 = ((f32[128,1,4096]{2,1,0:T(1,128)}), f32[128,1,4096]{2,1,0:T(1,128)}, u32[]{:S(2)}, u32[]{:S(2)}) async-start(f32[128,1,4096]{2,1,0:T(1,128)} %copy.34), calls=%async_computation.1 | async-start | bytes 4194304 | tf_op jit(solution)/shard_map/all_to_all | solution.py:63
  235.4 50.2 %collective-permute-start.2 = (f32[67,256]{1,0:T(8,128)S(1)}, f32[67,256]{1,0:T(8,128)S(1)}, u32[]{:S(2)}, u32[]{:S(2)}) collective-permute-start(f32[67,256]{1,0:T(8,128)S(1)} %get-tuple-element.79), channel_id=1, source_target_pairs={{0,1},{1,2},{2,3},{3,4},{4,5},{5,6},{6,7},{7,8},{8,9},{9,10},{10,1... | collective-permute-start | bytes 205832 | tf_op jit(solution)/shard_map/ppermute | solution.py:15
  238.0 47.6 %collective-permute-start.3 = (f32[67,256]{1,0:T(8,128)S(1)}, f32[67,256]{1,0:T(8,128)S(1)}, u32[]{:S(2)}, u32[]{:S(2)}) collective-permute-start(f32[67,256]{1,0:T(8,128)S(1)} %get-tuple-element.80), channel_id=1, source_target_pairs={{1,0},{2,1},{3,2},{4,3},{5,4},{6,5},{7,6},{8,7},{9,8},{10,9},{11,1... | collective-permute-start | bytes 205832 | tf_op jit(solution)/shard_map/ppermute | solution.py:18
  297.5 29.0 %copy-start.6 = (f32[4,64,256]{2,1,0:T(8,128)}, f32[4,64,256]{2,1,0:T(8,128)S(1)}, u32[]{:S(2)}) copy-start(f32[4,64,256]{2,1,0:T(8,128)S(1)} %get-tuple-element.50) | copy-start | bytes 786436
  331.8 4.0 %copy-start.5 = (f32[1,128,16,64]{1,3,2,0:T(8,128)S(1)}, f32[1,128,16,64]{1,3,2,0:T(8,128)}, u32[]{:S(2)}) copy-start(f32[1,128,16,64]{1,3,2,0:T(8,128)} %param.20) | copy-start | bytes 1572868
  359.7 5.6 %copy-start.11 = (s32[1024]{0:T(1024)S(1)}, s32[1024]{0:T(1024)}, u32[]{:S(2)}) copy-start(s32[1024]{0:T(1024)} %get-tuple-element.84) | copy-start | bytes 12292
  359.7 9.5 %copy-start.9 = (f32[4,64,64]{2,1,0:T(8,128)S(1)}, f32[4,64,64]{2,1,0:T(8,128)}, u32[]{:S(2)}) copy-start(f32[4,64,64]{2,1,0:T(8,128)} %param.18) | copy-start | bytes 196612
Sparse Core Ops, SparseCore 0:
  27.1 122.4 all-gather.2
  211.6 114.9 all-gather.4
where the time goes:
time: 381 us; the launch traced here: 379 us
  waiting for transfers between devices  139 us (36%)
  local copies, waits for them, and re-layouts  79.5 us (21%)
  blocking collectives  67.9 us (18%)
  starting transfers between devices  47.8 us (13%)
  matrix products  18.6 us (5%)
  between operations  13.8 us (4%)
  loops' own time  10.3 us (3%)
    ppermute x2, waiting for transfers between devices, extended(): lax.ppermute(lax.slice_in_dim(block, block.shape[dim] - width, None, axis...  77.3 us
    all_gather x2, waiting for transfers between devices, one_product(): lax.all_gather(parent[None], 'leaf', axis=0, tiled=True)  61.6 us
    psum x2, blocking collectives, one_product(): top_term = lax.psum(top_partial, 'sub')  35.2 us
    psum x2, blocking collectives, one_product(): parent = lax.psum(parent_part, 'sub')  32.7 us
    all_to_all x2, starting transfers between devices, one_product(): lax.all_to_all(outgoing.reshape(slot_total, rhs_count * rank), 'leaf', sp...  28.2 us
    all_to_all x4, local copies, waits for them, and re-layouts, one_product(): lax.all_to_all(outgoing.reshape(slot_total, rhs_count * rank), 'leaf', sp...  21 us
    ppermute x2, starting transfers between devices, extended(): lax.ppermute(lax.slice_in_dim(block, 0, width, axis=dim), axis, backward)  15 us
    gather x4, local copies, waits for them, and re-layouts, one_product(): outgoing = skeleton[send_leaf.reshape(-1)]  14.2 us
  transfers between devices with their start and end apart: 8, of which 4 were waited for; matrix products, arithmetic and copies ran while one was open for 16% of the time, Pallas kernels for 0%

commit v1 on v0

--- a/solution.py
+++ b/solution.py
@@ -89,7 +89,17 @@
         lax.all_gather(parent[None], "leaf", axis=0, tiled=True), row_start, quarter, 2
     )
     top_partial = add_top(rows, coupling_rows)
-    top_term = lax.psum(top_partial, "sub")
+
+    def arrange_runs_now(shard_in, dev_axis):
+        axis_n = jax.lax.axis_size(dev_axis)
+        r1 = shard_in
+        for u in [ix for ix in (1, 2, 4, 8, 16) if ix < axis_n]:
+            r1 = r1 + jax.lax.ppermute(
+                r1, axis_name=dev_axis, perm=list(map(lambda idx: (idx, idx ^ u), range(axis_n)))
+            )
+        return r1
+
+    top_term = arrange_runs_now(top_partial, "sub")
     coef = far + jnp.einsum("pr,lrq->lpq", top_term, down_transfer, precision=highest)
     total = near + jnp.einsum("lpr,lra->lpa", coef, basis, precision=highest)
     return total.transpose(1, 0, 2).reshape(rhs_count, leaf_count * leaf_size)

time: 381 us -> 414 us (1.087)
  the two profiles are of different devices: /device:TPU:16 before, /device:TPU:1 now
where the time goes in v1:
time: 414 us; the launch traced here: 412 us
  waiting for transfers between devices  170 us (41%)
  local copies, waits for them, and re-layouts  93.2 us (23%)
  starting transfers between devices  64.8 us (16%)
  blocking collectives  28.5 us (7%)
  matrix products  24.8 us (6%)
  between operations  13.9 us (3%)
  loops' own time  11 us (3%)
  other arithmetic  5.55 us (1%)
    all_gather x2, waiting for transfers between devices, one_product(): lax.all_gather(parent[None], 'leaf', axis=0, tiled=True)  167 us
    all_to_all x2, starting transfers between devices, one_product(): lax.all_to_all(outgoing.reshape(slot_total, rhs_count * rank), 'leaf', sp...  36.3 us
    psum x2, blocking collectives, one_product(): parent = lax.psum(parent_part, 'sub')  28.5 us
    all_to_all x4, local copies, waits for them, and re-layouts, one_product(): lax.all_to_all(outgoing.reshape(slot_total, rhs_count * rank), 'leaf', sp...  21.2 us
    ppermute x4, starting transfers between devices, arrange_runs_now(): jax.lax.ppermute(r1, axis_name=dev_axis, perm=list(map(lambda idx: (idx,...  15 us
    dot_general x8, matrix products, near_leaf(): jnp.dot(window[:rhs_count], kernels, precision=highest, preferred_element...  14.7 us
    gather x4, local copies, waits for them, and re-layouts, one_product(): outgoing = skeleton[send_leaf.reshape(-1)]  14.3 us
    reshape x2, local copies, waits for them, and re-layouts, far_terms(): gathered = incoming.reshape(-1, rows, rank)[list_slot]  11.3 us
  transfers between devices with their start and end apart: 12, of which 6 were waited for; matrix products, arithmetic and copies ran while one was open for 28% of the time, Pallas kernels for 0%

profile of v1, /device:TPU:1, one launch (start us, length us, event | category | flops | bytes accessed | tf_op | source)
XLA Modules:
  0.0 411.6 jit_solution(12800602765645240326)
XLA Ops:
  6.5 1.5 fusion.52
  8.0 1.2 convolution_bitcast_fusion.9
  9.2 15.1 %psum.14 = f32[1,64,64]{2,1,0:T(8,128)} all-reduce(f32[1,64,64]{2,1,0:T(8,128)S(1)} %convolution_bitcast_fusion.9), channel_id=1, replica_groups=mesh['leaf'=128,'sub'=4] {'sub'}, use_global_device_ids=true, to_apply=%region_2.3 | all-reduce | flops 4096 | bytes 32768 | tf_op jit(solution)/shard_map/psum | solution.py:86
  25.6 2.8 gather_fusion
  28.4 3.8 copy.31
  32.2 4.1 copy.32
  36.3 21.5 %all-to-all-start = ((f32[128,1,4096]{2,1,0:T(1,128)}), f32[128,1,4096]{2,1,0:T(1,128)}, u32[]{:S(2)}, u32[]{:S(2)}) async-start(f32[128,1,4096]{2,1,0:T(1,128)} %copy.32), calls=%async_computation | async-start | bytes 4194304 | tf_op jit(solution)/shard_map/all_to_all | solution.py:63
  57.9 1.9 collective-permute-start
  59.8 4.9 %collective-permute-start.1 = (f32[67,256]{1,0:T(8,128)S(1)}, f32[67,256]{1,0:T(8,128)S(1)}, u32[]{:S(2)}, u32[]{:S(2)}) collective-permute-start(f32[67,256]{1,0:T(8,128)S(1)} %get-tuple-element.82), channel_id=1, source_target_pairs={{1,0},{2,1},{3,2},{4,3},{5,4},{6,5},{7,6},{8,7},{9,8},{10,9},{11,1... | collective-permute-start | bytes 205832 | tf_op jit(solution)/shard_map/ppermute | solution.py:18
  66.2 0.8 pad_maximum_fusion
  67.0 84.4 %all-gather.3.cloned.1.call-done = f32[128,64,64]{2,1,0:T(8,128)} async-done(((f32[1,64,64]{2,1,0:T(8,128)}), f32[128,64,64]{2,1,0:T(8,128)}) %all-gather.3.cloned.1.call-update) | async-done | bytes 2097168 | tf_op jit(solution)/shard_map/all_gather | solution.py:89
  151.3 5.3 %constant_dynamic-slice_fusion.3 = f32[128,64,16]{2,1,0:T(8,128)} fusion(f32[128,64,64]{2,1,0:T(8,128)} %all-gather.3.cloned.1.call-done, s32[]{:T(128)S(6)} %select_n.38), kind=kLoop, calls=%fused_computation.101 | loop fusion | bytes 1048580 | tf_op jit(solution)/shard_map/dynamic_slice | solution.py:88
  156.7 4.0 copy.45
  160.7 1.2 convolution_bitcast_fusion.8
  161.9 3.1 collective-permute-start.2
  165.0 22.3 %while.20 = (s32[]{:T(128)}, f32[4,64,256]{2,1,0:T(8,128)S(1)}, s32[4]{0:T(128)S(1)}, f32[67,1536]{1,0:T(8,128)}, s32[]{:T(128)}, /*index=5*/s32[1]{0:T(128)}, s...) while((s32[]{:T(128)}, f32[4,64,256]{2,1,0:T(8,128)S(1)}, s32[4]{0:T(128)S(1)}, ...), condition=%wide.region_1.2_spmd, body=%wide.region_0.1_spmd.sunk | while | flops 152961040 | bytes 339797 | solution.py:82
  166.2 0.8 slice.92
  167.8 1.0 dynamic-slice_reduce_fusion.8
  168.7 1.8 fusion.93
  173.4 1.0 dynamic-slice_reduce_fusion.8
  174.3 1.8 fusion.93
  177.4 0.8 slice.92
  178.9 1.0 dynamic-slice_reduce_fusion.8
  179.9 1.8 fusion.93
  183.0 0.8 slice.92
  184.5 1.0 dynamic-slice_reduce_fusion.8
  185.5 1.8 fusion.93
  187.4 5.7 %copy.33 = f32[128,1,4096]{0,2,1:T(8,128)} copy(f32[128,1,4096]{2,1,0:T(1,128)} %all-to-all-done) | data formatting | bytes 4194304 | tf_op jit(solution)/shard_map/all_to_all | solution.py:63
  193.1 5.6 %copy.34 = f32[128,64,64]{2,1,0:T(8,128)} copy(f32[128,64,64]{0,2,1:T(8,128)} %bitcast.123) | data formatting | bytes 4194304 | tf_op jit(solution)/shard_map/reshape | solution.py:36
  198.7 2.9 gather_fusion.1
  201.7 0.8 add.93
  202.5 4.5 %collective-permute-start.3 = (f32[64,64]{1,0:T(8,128)S(1)}, f32[64,64]{1,0:T(8,128)S(1)}, u32[]{:S(2)}, u32[]{:S(2)}) collective-permute-start(f32[64,64]{1,0:T(8,128)S(1)} %add.93), channel_id=1, source_target_pairs={{0,2},{1,3},{2,0},{3,1},{4,6},{5,7},{6,4},{7,5},{8,10},{9,11},{10,... | collective-permute-start | bytes 49160 | tf_op jit(solution)/shard_map/ppermute | solution.py:97
  207.0 1.1 convolution_bitcast_fusion.5
  209.3 1.3 fusion.55
  211.0 13.4 %psum.15 = f32[1,64,64]{2,1,0:T(8,128)} all-reduce(f32[1,64,64]{2,1,0:T(8,128)S(1)} %convolution_bitcast_fusion.7), channel_id=1, replica_groups=mesh['leaf'=128,'sub'=4] {'sub'}, use_global_device_ids=true, to_apply=%region_5.6 | all-reduce | flops 4096 | bytes 32768 | tf_op jit(solution)/shard_map/psum | solution.py:86
  224.4 2.9 gather_fusion.3
  227.3 4.8 %copy.37 = f32[128,64,64]{0,2,1:T(8,128)} copy(f32[128,64,64]{2,1,0:T(8,128)} %gather_fusion.3) | data formatting | bytes 4194304 | tf_op jit(solution)/shard_map/gather | solution.py:60
  232.1 5.7 %copy.38 = f32[128,1,4096]{2,1,0:T(1,128)} copy(f32[128,1,4096]{0,2,1:T(8,128)} %bitcast.124) | data formatting | bytes 4194304 | tf_op jit(solution)/shard_map/all_to_all | solution.py:63
  237.8 14.8 %all-to-all-start.1 = ((f32[128,1,4096]{2,1,0:T(1,128)}), f32[128,1,4096]{2,1,0:T(1,128)}, u32[]{:S(2)}, u32[]{:S(2)}) async-start(f32[128,1,4096]{2,1,0:T(1,128)} %copy.38), calls=%async_computation.1 | async-start | bytes 4194304 | tf_op jit(solution)/shard_map/all_to_all | solution.py:63
  252.8 1.9 collective-permute-start.4
  254.7 4.9 %collective-permute-start.5 = (f32[67,256]{1,0:T(8,128)S(1)}, f32[67,256]{1,0:T(8,128)S(1)}, u32[]{:S(2)}, u32[]{:S(2)}) collective-permute-start(f32[67,256]{1,0:T(8,128)S(1)} %get-tuple-element.80), channel_id=1, source_target_pairs={{1,0},{2,1},{3,2},{4,3},{5,4},{6,5},{7,6},{8,7},{9,8},{10,9},{11,1... | collective-permute-start | bytes 205832 | tf_op jit(solution)/shard_map/ppermute | solution.py:18
  260.1 0.9 collective-permute-done.5
  261.0 0.8 pad_maximum_fusion.1
  261.8 82.7 %all-gather.5.cloned.1.call-done = f32[128,64,64]{2,1,0:T(8,128)} async-done(((f32[1,64,64]{2,1,0:T(8,128)}), f32[128,64,64]{2,1,0:T(8,128)}) %all-gather.5.cloned.1.call-update) | async-done | bytes 2097168 | tf_op jit(solution)/shard_map/all_gather | solution.py:89
  344.5 5.3 %constant_dynamic-slice_fusion.2 = f32[128,64,16]{2,1,0:T(8,128)} fusion(f32[128,64,64]{2,1,0:T(8,128)} %all-gather.5.cloned.1.call-done, s32[]{:T(128)S(6)} %select_n.38), kind=kLoop, calls=%fused_computation.100 | loop fusion | bytes 1048580 | tf_op jit(solution)/shard_map/dynamic_slice | solution.py:88
  349.8 4.0 copy.46
  353.9 1.2 convolution_bitcast_fusion.6
  355.0 3.1 collective-permute-start.6
  358.2 23.0 %while.21 = (s32[]{:T(128)}, f32[4,64,256]{2,1,0:T(8,128)S(1)}, s32[4]{0:T(128)S(1)}, f32[67,1536]{1,0:T(8,128)}, s32[]{:T(128)}, /*index=5*/s32[1]{0:T(128)}, s...) while((s32[]{:T(128)}, f32[4,64,256]{2,1,0:T(8,128)S(1)}, s32[4]{0:T(128)S(1)}, ...), condition=%wide.region_4.5_spmd, body=%wide.region_3.4_spmd.sunk | while | flops 152961040 | bytes 339797 | solution.py:82
  359.6 0.8 slice.93
  361.1 1.0 dynamic-slice_reduce_fusion.9
  362.1 1.8 fusion.96
  366.9 1.0 dynamic-slice_reduce_fusion.9
  367.8 1.8 fusion.96
  372.6 1.0 dynamic-slice_reduce_fusion.9
  373.6 1.8 fusion.96
  378.4 1.0 dynamic-slice_reduce_fusion.9
  379.4 1.8 fusion.96
  381.2 5.7 %copy.39 = f32[128,1,4096]{0,2,1:T(8,128)} copy(f32[128,1,4096]{2,1,0:T(1,128)} %all-to-all-done.1) | data formatting | bytes 4194304 | tf_op jit(solution)/shard_map/all_to_all | solution.py:63
  387.0 5.6 %copy.40 = f32[128,64,64]{2,1,0:T(8,128)} copy(f32[128,64,64]{0,2,1:T(8,128)} %bitcast.125) | data formatting | bytes 4194304 | tf_op jit(solution)/shard_map/reshape | solution.py:36
  392.6 2.8 gather_fusion.4
  396.2 4.3 %collective-permute-start.7 = (f32[64,64]{1,0:T(8,128)S(1)}, f32[64,64]{1,0:T(8,128)S(1)}, u32[]{:S(2)}, u32[]{:S(2)}) collective-permute-start(f32[64,64]{1,0:T(8,128)S(1)} %add.97), channel_id=1, source_target_pairs={{0,2},{1,3},{2,0},{3,1},{4,6},{5,7},{6,4},{7,5},{8,10},{9,11},{10,... | collective-permute-start | bytes 49160 | tf_op jit(solution)/shard_map/ppermute | solution.py:97
  400.5 1.1 convolution_bitcast_fusion.4
  403.0 1.0 add_bitcast_fusion
  (92 shorter events, 16.7 us)
Async XLA Ops:
  6.5 59.0 %copy-start = (f32[32,64,64]{2,1,0:T(8,128)S(1)}, f32[32,64,64]{2,1,0:T(8,128)}, u32[]{:S(2)}) copy-start(f32[32,64,64]{2,1,0:T(8,128)} %param.19) | copy-start | bytes 1572868
  6.5 144.8 %all-gather.3.cloned.1.call-start = ((), (), s32[]{:S(2)}) async-start(), calls=%async_computation.2 | async-start | bytes 4227072 | tf_op jit(solution)/shard_map/all_gather | solution.py:89
  25.0 0.6 copy-start.13
  32.2 25.6 %copy-start.7 = (f32[64,1024]{1,0:T(8,128)S(1)}, f32[64,1024]{1,0:T(8,128)}, u32[]{:S(2)}) copy-start(f32[64,1024]{1,0:T(8,128)} %param.14) | copy-start | bytes 786436
  32.2 25.7 %copy-start.11 = (f32[3,1024]{1,0:T(4,128)S(1)}, f32[3,1024]{1,0:T(4,128)}, u32[]{:S(2)}) copy-start(f32[3,1024]{1,0:T(4,128)} %param.15) | copy-start | bytes 36868
  32.2 32.5 %copy-start.14 = (s32[4,8]{1,0:T(4,128)S(1)}, s32[4,8]{1,0:T(4,128)}, u32[]{:S(2)}) copy-start(s32[4,8]{1,0:T(4,128)} %param.22) | copy-start | bytes 388
  32.2 32.6 %copy-start.15 = (s32[4,8]{1,0:T(4,128)S(1)}, s32[4,8]{1,0:T(4,128)}, u32[]{:S(2)}) copy-start(s32[4,8]{1,0:T(4,128)} %param.23) | copy-start | bytes 388
  36.3 151.0 %all-to-all-start = ((f32[128,1,4096]{2,1,0:T(1,128)}), f32[128,1,4096]{2,1,0:T(1,128)}, u32[]{:S(2)}, u32[]{:S(2)}) async-start(f32[128,1,4096]{2,1,0:T(1,128)} %copy.32), calls=%async_computation | async-start | bytes 4194304 | tf_op jit(solution)/shard_map/all_to_all | solution.py:63
  57.8 286.7 %all-gather.5.cloned.1.call-start = ((), (), s32[]{:S(2)}) async-start(), calls=%async_computation.3 | async-start | bytes 4227072 | tf_op jit(solution)/shard_map/all_gather | solution.py:89
  57.9 8.2 %collective-permute-start = (f32[67,256]{1,0:T(8,128)S(1)}, f32[67,256]{1,0:T(8,128)S(1)}, u32[]{:S(2)}, u32[]{:S(2)}) collective-permute-start(f32[67,256]{1,0:T(8,128)S(1)} %get-tuple-element.81), channel_id=1, source_target_pairs={{0,1},{1,2},{2,3},{3,4},{4,5},{5,6},{6,7},{7,8},{8,9},{9,10},{10,1... | collective-permute-start | bytes 205832 | tf_op jit(solution)/shard_map/ppermute | solution.py:15
  59.8 6.3 %collective-permute-start.1 = (f32[67,256]{1,0:T(8,128)S(1)}, f32[67,256]{1,0:T(8,128)S(1)}, u32[]{:S(2)}, u32[]{:S(2)}) collective-permute-start(f32[67,256]{1,0:T(8,128)S(1)} %get-tuple-element.82), channel_id=1, source_target_pairs={{1,0},{2,1},{3,2},{4,3},{5,4},{6,5},{7,6},{8,7},{9,8},{10,9},{11,1... | collective-permute-start | bytes 205832 | tf_op jit(solution)/shard_map/ppermute | solution.py:18
  156.7 4.0 copy-start.4
  161.9 39.8 %collective-permute-start.2 = (f32[64,64]{1,0:T(8,128)}, f32[64,64]{1,0:T(8,128)}, u32[]{:S(2)}, u32[]{:S(2)}) collective-permute-start(f32[64,64]{1,0:T(8,128)} %convolution_bitcast_fusion.8), channel_id=1, source_target_pairs={{0,1},{1,0},{2,3},{3,2},{4,5},{5,4},{6,7},{7,6},{8,9},{9,8},{10,11... | collective-permute-start | bytes 49160 | tf_op jit(solution)/shard_map/ppermute | solution.py:97
  187.3 11.4 %copy-start.2 = (f32[4,64,256]{2,1,0:T(8,128)}, f32[4,64,256]{2,1,0:T(8,128)S(1)}, u32[]{:S(2)}) copy-start(f32[4,64,256]{2,1,0:T(8,128)S(1)} %get-tuple-element.49) | copy-start | bytes 786436
  193.1 15.6 %copy-start.8 = (f32[4,64,64]{2,1,0:T(8,128)S(1)}, f32[4,64,64]{2,1,0:T(8,128)}, u32[]{:S(2)}) copy-start(f32[4,64,64]{2,1,0:T(8,128)} %param.18) | copy-start | bytes 196612
  193.1 15.9 %copy-start.1 = (f32[4,64,256]{2,1,0:T(8,128)S(1)}, f32[4,64,256]{2,1,0:T(8,128)}, u32[]{:S(2)}) copy-start(f32[4,64,256]{2,1,0:T(8,128)} %param.16) | copy-start | bytes 786436
  201.7 9.0 %copy-start.10 = (f32[4,64,64]{2,1,0:T(8,128)S(1)}, f32[4,64,64]{2,1,0:T(8,128)}, u32[]{:S(2)}) copy-start(f32[4,64,64]{2,1,0:T(8,128)} %param.17) | copy-start | bytes 196612
  202.5 6.2 %collective-permute-start.3 = (f32[64,64]{1,0:T(8,128)S(1)}, f32[64,64]{1,0:T(8,128)S(1)}, u32[]{:S(2)}, u32[]{:S(2)}) collective-permute-start(f32[64,64]{1,0:T(8,128)S(1)} %add.93), channel_id=1, source_target_pairs={{0,2},{1,3},{2,0},{3,1},{4,6},{5,7},{6,4},{7,5},{8,10},{9,11},{10,... | collective-permute-start | bytes 49160 | tf_op jit(solution)/shard_map/ppermute | solution.py:97
  232.1 20.5 %copy-start.3 = (f32[4,64,256]{2,1,0:T(8,128)S(1)}, f32[4,64,256]{2,1,0:T(8,128)}, u32[]{:S(2)}) copy-start(f32[4,64,256]{2,1,0:T(8,128)} %copy-done.2) | copy-start | bytes 786436
  237.8 143.4 %all-to-all-start.1 = ((f32[128,1,4096]{2,1,0:T(1,128)}), f32[128,1,4096]{2,1,0:T(1,128)}, u32[]{:S(2)}, u32[]{:S(2)}) async-start(f32[128,1,4096]{2,1,0:T(1,128)} %copy.38), calls=%async_computation.1 | async-start | bytes 4194304 | tf_op jit(solution)/shard_map/all_to_all | solution.py:63
  252.8 7.3 %collective-permute-start.4 = (f32[67,256]{1,0:T(8,128)S(1)}, f32[67,256]{1,0:T(8,128)S(1)}, u32[]{:S(2)}, u32[]{:S(2)}) collective-permute-start(f32[67,256]{1,0:T(8,128)S(1)} %get-tuple-element.79), channel_id=1, source_target_pairs={{0,1},{1,2},{2,3},{3,4},{4,5},{5,6},{6,7},{7,8},{8,9},{9,10},{10,1... | collective-permute-start | bytes 205832 | tf_op jit(solution)/shard_map/ppermute | solution.py:15
  254.7 6.2 %collective-permute-start.5 = (f32[67,256]{1,0:T(8,128)S(1)}, f32[67,256]{1,0:T(8,128)S(1)}, u32[]{:S(2)}, u32[]{:S(2)}) collective-permute-start(f32[67,256]{1,0:T(8,128)S(1)} %get-tuple-element.80), channel_id=1, source_target_pairs={{1,0},{2,1},{3,2},{4,3},{5,4},{6,5},{7,6},{8,7},{9,8},{10,9},{11,1... | collective-permute-start | bytes 205832 | tf_op jit(solution)/shard_map/ppermute | solution.py:18
  349.8 4.0 copy-start.5
  355.0 40.4 %collective-permute-start.6 = (f32[64,64]{1,0:T(8,128)}, f32[64,64]{1,0:T(8,128)}, u32[]{:S(2)}, u32[]{:S(2)}) collective-permute-start(f32[64,64]{1,0:T(8,128)} %convolution_bitcast_fusion.6), channel_id=1, source_target_pairs={{0,1},{1,0},{2,3},{3,2},{4,5},{5,4},{6,7},{7,6},{8,9},{9,8},{10,11... | collective-permute-start | bytes 49160 | tf_op jit(solution)/shard_map/ppermute | solution.py:97
  381.2 5.8 %copy-start.6 = (f32[4,64,256]{2,1,0:T(8,128)}, f32[4,64,256]{2,1,0:T(8,128)S(1)}, u32[]{:S(2)}) copy-start(f32[4,64,256]{2,1,0:T(8,128)S(1)} %get-tuple-element.50) | copy-start | bytes 786436
  387.0 5.6 %copy-start.12 = (s32[1024]{0:T(1024)S(1)}, s32[1024]{0:T(1024)}, u32[]{:S(2)}) copy-start(s32[1024]{0:T(1024)} %get-tuple-element.84) | copy-start | bytes 12292
  387.0 15.4 %copy-start.9 = (f32[4,64,64]{2,1,0:T(8,128)S(1)}, f32[4,64,64]{2,1,0:T(8,128)}, u32[]{:S(2)}) copy-start(f32[4,64,64]{2,1,0:T(8,128)} %param.18) | copy-start | bytes 196612
  396.2 6.2 %collective-permute-start.7 = (f32[64,64]{1,0:T(8,128)S(1)}, f32[64,64]{1,0:T(8,128)S(1)}, u32[]{:S(2)}, u32[]{:S(2)}) collective-permute-start(f32[64,64]{1,0:T(8,128)S(1)} %add.97), channel_id=1, source_target_pairs={{0,2},{1,3},{2,0},{3,1},{4,6},{5,7},{6,4},{7,5},{8,10},{9,11},{10,... | collective-permute-start | bytes 49160 | tf_op jit(solution)/shard_map/ppermute | solution.py:97
Sparse Core Ops, SparseCore 0:
  24.5 126.8 all-gather.2
  224.5 119.9 all-gather.4
